TPU v7x, 256 devices: a whole 4x4x8 slice. The times are simulated.
256 devices in a mesh: req: 64 (over x, z, core), tp: 4 (over y).
Axes of the slice: x: 4, y: 4, z: 8, core: 2. Of those that a mesh axis runs over, the one named last changes fastest.
Arguments:
- queries: bfloat16 [512, 2560], P('req', 'tp'), may hold values from -68 to 68, as said below
- new_kv: bfloat16 [512, 4, 256], P('req', 'tp'), may hold values from -6 to 6
- residual: bfloat16 [512, 2560], P('req', 'tp'), may hold values from -6 to 6
- kv_cache: bfloat16 [512, 512, 4, 256], P('req', None, 'tp'), may hold values from -6 to 6
- cache_len: int32 [512], P('req'), may hold values from 1 to 511, as said below
- request_perm: int32 [512], replicated, may hold values from 0 to 511, each once
- expert_ids: int32 [512, 6], P('req'), may hold values from 0 to 63, all different within a row; in each aligned block of 8 rows (0 to 7, 8 to 15, ...) at most 2 rows name the same one
- route_wt: float32 [512, 6], P('req'), may hold values from 0.05 to 1
- attn_out_w: bfloat16 [2560, 2560], P('tp'), may hold values from -0.125 to 0.125
- post_gain: float32 [2560], replicated, may hold values from 0.25 to 1.75
- expert_gate_up: bfloat16 [64, 2, 2560, 1536], P('req', None, None, 'tp'), may hold values from -0.125 to 0.125
- expert_down: bfloat16 [64, 1536, 2560], P('req', 'tp'), may hold values from -0.15625 to 0.15625
- final_gain: float32 [2560], replicated, may hold values from 0.25 to 1.75
- vocab_w: bfloat16 [103424, 2560], P(('req', 'tp')), may hold values from -0.125 to 0.125
Outputs:
- hidden_out: bfloat16 [512, 2560], P('req', 'tp')
- state_norm: float32 [512], P('req')
- top_logit: float32 [512], P('req')
Inputs may be any that keep to these rules, and one draw needn't show every extreme that they name: queries lie within this range. Slot s holds cache_len[s] filled rows; some slot holds exactly 511. `request_perm`: a permutation of the slots. `expert_ids`: each row names 6 different experts; among the rows of one device (aligned blocks of 8 rows) no expert is named more than 2 times, and in some block one expert is named exactly 2 times.
All inputs are finite; a program needn't handle non-finite values.
Results may differ from a plain program's by a relative error of at most 0.007.
Values may be sent and summed in bfloat16 or wider, within the bound.
No kernel may reach another device: no remote copies, remote signals or barrier semaphores. Data moves between devices by JAX's collectives and lax.ppermute only.
A program may use at most 64 MiB of HBM per device.

v0:
```python
import jax
import jax.numpy as jnp
from jax import lax
from jax.sharding import PartitionSpec as P

epsilon = 1e-05


def attend(queries, fresh_kv, kv_block, lengths, head_dim):
    slot_count, context, kv_heads, _ = kv_block.shape
    groups = queries.shape[1] // head_dim // kv_heads
    query_heads = queries.reshape(slot_count, kv_heads, groups, head_dim)
    key_part = kv_block[..., :head_dim]
    value_part = kv_block[..., head_dim:]
    score_scale = head_dim ** (-0.5)
    scores = (
        jnp.einsum("skgd,sckd->skgc", query_heads, key_part, preferred_element_type=jnp.float32)
        * score_scale
    )
    live_mask = (jnp.arange(context, dtype=jnp.int32)[None, :] < lengths[:, None])[:, None, None, :]
    scores = jnp.where(live_mask, scores, -1e30)
    own_score = (
        jnp.einsum(
            "skgd,skd->skg",
            query_heads,
            fresh_kv[..., :head_dim],
            preferred_element_type=jnp.float32,
        )
        * score_scale
    )
    highest = jnp.maximum(jnp.max(scores, axis=-1), own_score)
    weights = jnp.where(live_mask, jnp.exp(scores - highest[..., None]), 0.0)
    own_weight = jnp.exp(own_score - highest)
    total_weight = jnp.sum(weights, axis=-1) + own_weight
    own_round = lax.optimization_barrier(own_weight.astype(jnp.bfloat16)).astype(jnp.float32)
    mixed_sum = jnp.einsum(
        "skgc,sckd->skgd",
        weights.astype(jnp.bfloat16),
        value_part,
        preferred_element_type=jnp.float32,
    )
    mixed_sum = mixed_sum + own_round[..., None] * fresh_kv[:, :, None, head_dim:].astype(
        jnp.float32
    )
    return (mixed_sum / total_weight[..., None]).reshape(slot_count, -1).astype(jnp.bfloat16)


def expert_rows(inputs, gate_up, down_proj):
    gate_val = jnp.dot(inputs, gate_up[0], preferred_element_type=jnp.float32)
    upward = jnp.dot(inputs, gate_up[1], preferred_element_type=jnp.float32)
    active = (jax.nn.silu(gate_val) * upward).astype(jnp.bfloat16)
    return jnp.dot(active, down_proj, preferred_element_type=jnp.float32)


def send_back(results):
    return lax.all_to_all(
        results.astype(jnp.bfloat16), "req", split_axis=0, concat_axis=0, tiled=True
    ).astype(results.dtype)


def on_device(
    queries,
    new_kv,
    residual,
    kv_cache,
    cache_len,
    request_perm,
    expert_ids,
    route_wt,
    attn_out_w,
    post_gain,
    expert_gate_up,
    expert_down,
    final_gain,
    vocab_w,
):
    group_count = lax.axis_size("req")
    group_index = lax.axis_index("req")
    member = lax.axis_index("tp")
    local_rows = queries.shape[0]
    top_count = expert_ids.shape[1]
    col_width = residual.shape[1]
    model_width = attn_out_w.shape[1]
    head_dim = new_kv.shape[2] // 2
    capacity = max(2, (local_rows * top_count + group_count - 1) // group_count)
    dealt_q, dealt_kv, dealt_res = (
        lax.all_gather(queries, "req", axis=0, tiled=True),
        lax.all_gather(new_kv, "req", axis=0, tiled=True),
        lax.all_gather(residual, "req", axis=0, tiled=True),
    )
    total_rows = dealt_q.shape[0]
    slot_ids = group_index * local_rows + jnp.arange(local_rows, dtype=jnp.int32)
    pick_rows = (request_perm[None, :] == slot_ids[:, None]).astype(jnp.bfloat16)
    mine_q = jnp.dot(pick_rows, dealt_q, preferred_element_type=jnp.float32).astype(jnp.bfloat16)
    mine_kv = jnp.dot(
        pick_rows, dealt_kv.reshape(total_rows, -1), preferred_element_type=jnp.float32
    )
    mine_kv = mine_kv.astype(jnp.bfloat16).reshape(new_kv.shape)
    mine_res = jnp.dot(pick_rows, dealt_res, preferred_element_type=jnp.float32)
    attended = attend(mine_q, mine_kv, kv_cache, cache_len, head_dim)
    partial_value = jnp.dot(attended, attn_out_w, preferred_element_type=jnp.float32)
    col_start = member * col_width
    own_part = lax.dynamic_slice_in_dim(partial_value, col_start, col_width, 1) + mine_res
    summand = lax.dynamic_update_slice_in_dim(partial_value, own_part, col_start, 1)
    mixed_full = lax.psum(summand, "tp")
    scale_rows = lax.rsqrt(jnp.mean(mixed_full * mixed_full, axis=1, keepdims=True) + epsilon)
    normed = (mixed_full * scale_rows * post_gain).astype(jnp.bfloat16)
    mixed_cols = lax.dynamic_slice_in_dim(mixed_full, col_start, col_width, 1)
    expert_axis = jnp.arange(group_count, dtype=jnp.int32)
    hit_table = (
        (expert_ids[..., None] == expert_axis)
        .astype(jnp.int32)
        .reshape(local_rows * top_count, group_count)
    )
    earlier = jnp.cumsum(hit_table, axis=0) - hit_table
    slot_rank = jnp.sum(earlier * hit_table, axis=1)
    target = expert_ids.reshape(-1) * capacity + slot_rank
    slot_axis = jnp.arange(group_count * capacity, dtype=jnp.int32)
    matches = (slot_axis[:, None] == target[None, :]).astype(jnp.float32)
    matches = matches.reshape(group_count * capacity, local_rows, top_count)
    route_share = route_wt / jnp.sum(route_wt, axis=1, keepdims=True)
    blending = jnp.sum(matches * route_share[None], axis=2).T
    gate_up = expert_gate_up[0]
    down_proj = expert_down[0]
    every_row = lax.all_gather(normed, "req", axis=0, tiled=True)
    every_id = lax.all_gather(expert_ids, "req", axis=0, tiled=True)
    all_hits = (every_id[..., None] == expert_axis).astype(jnp.int32)
    all_hits = all_hits.reshape(group_count, local_rows * top_count, group_count)
    all_prior = jnp.cumsum(all_hits, axis=1) - all_hits
    all_rank = jnp.sum(all_prior * all_hits, axis=2)
    own_routes = every_id.reshape(group_count, local_rows * top_count) == group_index
    cap_axis = jnp.arange(capacity, dtype=jnp.int32)
    chosen = (own_routes[..., None] & (all_rank[..., None] == cap_axis)).astype(jnp.float32)
    chosen = jnp.sum(chosen.reshape(group_count, local_rows, top_count, capacity), axis=2).astype(
        jnp.bfloat16
    )
    inbound = jnp.einsum(
        "btc,btd->bcd",
        chosen,
        every_row.reshape(group_count, local_rows, model_width),
        preferred_element_type=jnp.float32,
    )
    inbound = inbound.astype(jnp.bfloat16)
    produced = expert_rows(inbound.reshape(group_count * capacity, model_width), gate_up, down_proj)
    returned = send_back(produced.reshape(group_count, capacity, model_width))
    moe_part = jnp.dot(
        blending,
        returned.reshape(group_count * capacity, model_width),
        precision=lax.Precision.HIGHEST,
        preferred_element_type=jnp.float32,
    )
    moe_cols = lax.psum_scatter(
        moe_part.astype(jnp.bfloat16), "tp", scatter_dimension=1, tiled=True
    ).astype(jnp.float32)
    state_cols = (mixed_cols + moe_cols).astype(jnp.bfloat16)
    state_row = lax.all_gather(state_cols, "tp", axis=1, tiled=True)
    every_state = lax.all_gather(state_row, "req", axis=0, tiled=True)
    wanted = lax.dynamic_slice_in_dim(request_perm, group_index * local_rows, local_rows)
    back_pick = wanted[:, None] == jnp.arange(total_rows, dtype=jnp.int32)[None, :]
    own_rows = jnp.dot(
        back_pick.astype(jnp.bfloat16), every_state, preferred_element_type=jnp.float32
    )
    hidden_out = lax.dynamic_slice_in_dim(own_rows, col_start, col_width, 1).astype(jnp.bfloat16)
    state_norm = jnp.sqrt(jnp.mean(own_rows * own_rows, axis=1) + epsilon)
    every_flat = every_state.astype(jnp.float32)
    ready_rows = (
        every_flat
        * lax.rsqrt(jnp.mean(every_flat * every_flat, axis=1, keepdims=True) + epsilon)
        * final_gain
    ).astype(jnp.bfloat16)
    logits = lax.dot_general(
        ready_rows, vocab_w, (((1,), (1,)), ((), ())), preferred_element_type=jnp.float32
    )
    local_top = jnp.max(logits, axis=1)
    global_top = lax.pmax(local_top, ("req", "tp"))
    top_logit = jnp.sum(jnp.where(back_pick, global_top[None, :], 0.0), axis=1)
    return (hidden_out, state_norm, top_logit)


def solution(mesh):
    placed = (
        P("req", "tp"),
        P("req", "tp", None),
        P("req", "tp"),
        P("req", None, "tp", None),
        P("req"),
        P(),
        P("req", None),
        P("req", None),
        P("tp", None),
        P(),
        P("req", None, None, "tp"),
        P("req", "tp", None),
        P(),
        P(("req", "tp"), None),
    )
    return jax.shard_map(
        on_device,
        mesh=mesh,
        in_specs=placed,
        out_specs=(P("req", "tp"), P("req"), P("req")),
        check_vma=False,
    )
```

profile of v0, /device:TPU:1, one launch (start us, length us, event | category | flops | bytes accessed | tf_op | source)
XLA Modules:
  0.0 543.5 jit_solution(1999221724259459225)
XLA Ops:
  7.3 55.1 %all_gather.21 = bf16[512,640]{1,0:T(8,128)(2,1)S(1)} all-gather(bf16[8,640]{1,0:T(8,128)(2,1)} %param.14), channel_id=1, replica_groups=mesh['req'=64,'tp'=4] {'req'}, dimensions={0}, use_global_device_ids=true | all-gather | bytes 665600 | tf_op jit(solution)/shard_map/all_gather | solution.py:87
  62.4 43.1 %all_gather.22 = bf16[512,1,256]{2,0,1:T(8,128)(2,1)S(1)} all-gather(bf16[8,1,256]{2,0,1:T(8,128)(2,1)} %param.15), channel_id=1, replica_groups=mesh['req'=64,'tp'=4] {'req'}, dimensions={0}, use_global_device_ids=true | all-gather | bytes 266240 | tf_op jit(solution)/shard_map/all_gather | solution.py:88
  108.1 1.7 fusion.69
  110.0 52.5 %all_gather.23 = bf16[512,640]{1,0:T(8,128)(2,1)} all-gather(bf16[8,640]{1,0:T(8,128)(2,1)S(1)} %copy-done.7), channel_id=1, replica_groups=mesh['req'=64,'tp'=4] {'req'}, dimensions={0}, use_global_device_ids=true | all-gather | bytes 665600 | tf_op jit(solution)/shard_map/all_gather | solution.py:89
  166.7 40.7 %all-reduce.2.cloned.1.call-done = f32[8,2560]{1,0:T(8,128)} async-done(((f32[8,2560]{1,0:T(8,128)}), f32[8,2560]{1,0:T(8,128)}) %all-reduce.2.cloned.1.call-update) | async-done | bytes 81936 | tf_op jit(solution)/shard_map/psum | solution.py:105
  208.5 1.6 multiply_convert_fusion
  210.1 47.8 %all_gather.24 = s32[512,6]{1,0:T(8,128)S(1)} all-gather(s32[8,6]{1,0:T(8,128)S(1)} %copy-done.4), channel_id=1, replica_groups=mesh['req'=64,'tp'=4] {'req'}, dimensions={0}, use_global_device_ids=true | all-gather | bytes 12480 | tf_op jit(solution)/shard_map/all_gather | solution.py:126
  261.1 1.7 fusion.68
  262.9 28.5 %all-gather.3.cloned.1.call-done = bf16[512,2560]{1,0:T(8,128)(2,1)} async-done(((bf16[8,2560]{1,0:T(8,128)(2,1)}), bf16[512,2560]{1,0:T(8,128)(2,1)}) %all-gather.3.cloned.1.call-update) | async-done | bytes 2621456 | tf_op jit(solution)/shard_map/all_gather | solution.py:125
  291.4 3.4 convolution_convert_fusion
  294.8 2.7 reshape.188
  297.6 2.3 fusion.13
  299.9 2.1 fusion.26
  302.0 2.1 convolution_convert_fusion.1
  305.6 6.7 %all-to-all-start = ((bf16[64,2,2560]{2,1,0:T(2,128)(2,1)}), bf16[64,2,2560]{2,1,0:T(2,128)(2,1)}, u32[]{:S(2)}, u32[]{:S(2)}) async-start(bf16[64,2,2560]{2,1,0:T(2,128)(2,1)} %copy.46), calls=%async_computation | async-start | bytes 1310720 | tf_op jit(solution)/shard_map/all_to_all | solution.py:56
  313.3 19.0 %all-to-all-done = bf16[64,2,2560]{2,1,0:T(2,128)(2,1)} async-done(((bf16[64,2,2560]{2,1,0:T(2,128)(2,1)}), bf16[64,2,2560]{2,1,0:T(2,128)(2,1)}, u32[]{:S(2)}, u32[]{:S(2)}) %all-to-all-start) | async-done | bytes 655392 | tf_op jit(solution)/shard_map/all_to_all | solution.py:56
  332.4 2.7 reshape.189
  337.7 20.3 %reduce-scatter.4.cloned.1.call-done = bf16[640,8]{1,0:T(8,128)(2,1)} async-done(((bf16[2560,8]{1,0:T(8,128)(2,1)}), bf16[640,8]{1,0:T(8,128)(2,1)}) %reduce-scatter.4.cloned.1.call-update) | async-done | bytes 10256
  359.7 9.9 %all_gather.26 = bf16[8,2560]{1,0:T(8,128)(2,1)} all-gather(bf16[8,640]{1,0:T(8,128)(2,1)S(1)} %add_convert_fusion), channel_id=1, replica_groups=mesh['req'=64,'tp'=4] {'tp'}, dimensions={1}, use_global_device_ids=true | all-gather | bytes 51200 | tf_op jit(solution)/shard_map/all_gather | solution.py:156
  369.8 82.1 %all-gather.5.cloned.1.call-done = bf16[512,2560]{1,0:T(8,128)(2,1)} async-done(((bf16[8,2560]{1,0:T(8,128)(2,1)}), bf16[512,2560]{1,0:T(8,128)(2,1)}) %all-gather.5.cloned.1.call-update) | async-done | bytes 2621456 | tf_op jit(solution)/shard_map/all_gather | solution.py:157
  451.9 2.5 fusion
  454.4 3.0 fusion.20
  457.4 75.4 %pmax.7 = f32[512]{0:T(512)S(1)} all-reduce(f32[512]{0:T(512)S(1)} %fusion.20), channel_id=1, replica_groups=mesh['req'=64,'tp'=4] {'req','tp'}, use_global_device_ids=true, to_apply=%region_15.16 | all-reduce | flops 512 | bytes 4096 | tf_op jit(solution)/shard_map/pmax | solution.py:175
  533.5 2.3 multiply_reduce_fusion
  (73 shorter events, 20.3 us)
Async XLA Ops:
  7.2 156.9 %copy-start = (bf16[640,2560]{1,0:T(8,128)(2,1)S(1)}, bf16[640,2560]{1,0:T(8,128)(2,1)}, u32[]{:S(2)}) copy-start(bf16[640,2560]{1,0:T(8,128)(2,1)} %param.22) | copy-start | bytes 9830404
  7.2 102.8 %copy-start.7 = (bf16[8,640]{1,0:T(8,128)(2,1)S(1)}, bf16[8,640]{1,0:T(8,128)(2,1)}, u32[]{:S(2)}) copy-start(bf16[8,640]{1,0:T(8,128)(2,1)} %param.16) | copy-start | bytes 30724
  7.2 200.2 %all-reduce.2.cloned.1.call-start = ((), (), s32[]{:S(2)}) async-start(), calls=%async_computation.2 | async-start | bytes 163840 | tf_op jit(solution)/shard_map/psum | solution.py:105
  162.5 2.1 copy-start.8
  164.1 44.4 %copy-start.6 = (f32[2560]{0:T(1024)S(1)}, f32[2560]{0:T(1024)}, u32[]{:S(2)}) copy-start(f32[2560]{0:T(1024)} %param.23) | copy-start | bytes 30724
  164.1 46.0 %copy-start.4 = (s32[8,6]{1,0:T(8,128)S(1)}, s32[8,6]{1,0:T(8,128)}, u32[]{:S(2)}) copy-start(s32[8,6]{1,0:T(8,128)} %param.20) | copy-start | bytes 580
  166.0 0.6 copy-start.3
  166.6 124.8 %all-gather.3.cloned.1.call-start = ((), (), s32[]{:S(2)}) async-start(), calls=%async_computation.3 | async-start | bytes 2662400 | tf_op jit(solution)/shard_map/all_gather | solution.py:125
  297.5 2.3 copy-start.2
  302.0 10.9 %copy-start.5 = (f32[8,6]{1,0:T(8,128)S(1)}, f32[8,6]{1,0:T(8,128)}, u32[]{:S(2)}) copy-start(f32[8,6]{1,0:T(8,128)} %param.21) | copy-start | bytes 580
  305.6 26.7 %all-to-all-start = ((bf16[64,2,2560]{2,1,0:T(2,128)(2,1)}), bf16[64,2,2560]{2,1,0:T(2,128)(2,1)}, u32[]{:S(2)}, u32[]{:S(2)}) async-start(bf16[64,2,2560]{2,1,0:T(2,128)(2,1)} %copy.46), calls=%async_computation | async-start | bytes 1310720 | tf_op jit(solution)/shard_map/all_to_all | solution.py:56
  312.3 45.7 %reduce-scatter.4.cloned.1.call-start = ((), (), s32[]{:S(2)}) async-start(), calls=%async_computation.5 | async-start | bytes 819200
  336.5 117.8 %copy-start.9 = (f32[2560]{0:T(1024)S(1)}, f32[2560]{0:T(1024)}, u32[]{:S(2)}) copy-start(f32[2560]{0:T(1024)} %param.26) | copy-start | bytes 30724
  337.6 114.2 %all-gather.5.cloned.1.call-start = ((), (), s32[]{:S(2)}) async-start(), calls=%async_computation.4 | async-start | bytes 2662400 | tf_op jit(solution)/shard_map/all_gather | solution.py:157
  451.9 2.5 copy-start.1
Sparse Core Ops, SparseCore 0:
  166.8 40.6 all-reduce.1
  210.6 80.8 all-gather.2
  337.8 20.1 reduce-scatter.3
  369.8 82.0 all-gather.4
where the time goes:
time: 545 us; the launch traced here: 544 us
  blocking collectives  284 us (52%)
  waiting for transfers between devices  191 us (35%)
  matrix products  23.6 us (4%)
  between operations  14 us (3%)
  local copies, waits for them, and re-layouts  13.5 us (2%)
  other arithmetic  11 us (2%)
  starting transfers between devices  6.83 us (1%)
    all_gather x1, waiting for transfers between devices, on_device(): every_state = lax.all_gather(state_row, 'req', axis=0, tiled=True)  82.1 us
    pmax x1, blocking collectives, on_device(): global_top = lax.pmax(local_top, ('req', 'tp'))  75.4 us
    all_gather x1, blocking collectives, on_device(): lax.all_gather(queries, 'req', axis=0, tiled=True)  55.1 us
    all_gather x1, blocking collectives, on_device(): lax.all_gather(residual, 'req', axis=0, tiled=True)  52.5 us
    all_gather x1, blocking collectives, on_device(): every_id = lax.all_gather(expert_ids, 'req', axis=0, tiled=True)  47.8 us
    all_gather x1, blocking collectives, on_device(): lax.all_gather(new_kv, 'req', axis=0, tiled=True)  43.1 us
    psum x1, waiting for transfers between devices, on_device(): mixed_full = lax.psum(summand, 'tp')  40.7 us
    all_gather x1, waiting for transfers between devices, on_device(): every_row = lax.all_gather(normed, 'req', axis=0, tiled=True)  28.5 us
  transfers between devices with their start and end apart: 5, of which 5 were waited for; matrix products, arithmetic and copies ran while one was open for 1% of the time, Pallas kernels for 0%

commit v1 on v0

--- a/solution.py
+++ b/solution.py
@@ -4,6 +4,13 @@
 from jax.sharding import PartitionSpec as P
 
 epsilon = 1e-05
+
+
+def exchange_gather(array, name, dim):
+    size = lax.axis_size(name)
+    pieces = jnp.stack([array for _ in range(size)])
+    pieces = lax.all_to_all(pieces, name, split_axis=0, concat_axis=0)
+    return jnp.concatenate(pieces, axis=dim)
 
 
 def attend(queries, fresh_kv, kv_block, lengths, head_dim):
@@ -85,7 +92,7 @@
     capacity = max(2, (local_rows * top_count + group_count - 1) // group_count)
     dealt_q, dealt_kv, dealt_res = (
         lax.all_gather(queries, "req", axis=0, tiled=True),
-        lax.all_gather(new_kv, "req", axis=0, tiled=True),
+        exchange_gather(new_kv, "req", 0),
         lax.all_gather(residual, "req", axis=0, tiled=True),
     )
     total_rows = dealt_q.shape[0]

time: 545 us -> 513 us (0.941)
  blocking collectives: 284 us -> 239 us
  starting transfers between devices: 6.83 us -> 20 us
    all_gather x1 -> x0, blocking collectives: 43.1 us -> none  [on_device(): lax.all_gather(new_kv, 'req', axis=0, tiled=True)]
    all_to_all x0 -> x1, starting transfers between devices: none -> 13.2 us  [exchange_gather(): pieces = lax.all_to_all(pieces, name, split_axis=0, concat_axis=0)]
  transfers between devices with their start and end apart: 5 -> 6, of which waited for: 5 -> 5; matrix products, arithmetic and copies ran while one was open for 1% -> 2% of each run, Pallas kernels for 0% -> 0%
where the time goes in v1:
time: 513 us; the launch traced here: 512 us
  blocking collectives  239 us (47%)
  waiting for transfers between devices  191 us (37%)
  matrix products  22.2 us (4%)
  starting transfers between devices  20 us (4%)
  local copies, waits for them, and re-layouts  15 us (3%)
  between operations  14 us (3%)
  other arithmetic  10.4 us (2%)
    all_gather x1, waiting for transfers between devices, on_device(): every_state = lax.all_gather(state_row, 'req', axis=0, tiled=True)  82.3 us
    pmax x1, blocking collectives, on_device(): global_top = lax.pmax(local_top, ('req', 'tp'))  75.4 us
    all_gather x1, blocking collectives, on_device(): lax.all_gather(residual, 'req', axis=0, tiled=True)  53.9 us
    all_gather x1, blocking collectives, on_device(): lax.all_gather(queries, 'req', axis=0, tiled=True)  52.1 us
    all_gather x1, blocking collectives, on_device(): every_id = lax.all_gather(expert_ids, 'req', axis=0, tiled=True)  47.8 us
    psum x1, waiting for transfers between devices, on_device(): mixed_full = lax.psum(summand, 'tp')  41.7 us
    all_gather x1, waiting for transfers between devices, on_device(): every_row = lax.all_gather(normed, 'req', axis=0, tiled=True)  28.5 us
    unnamed x5, waiting for transfers between devices  19.8 us
  transfers between devices with their start and end apart: 6, of which 5 were waited for; matrix products, arithmetic and copies ran while one was open for 2% of the time, Pallas kernels for 0%

profile of v1, /device:TPU:1, one launch (start us, length us, event | category | flops | bytes accessed | tf_op | source)
XLA Modules:
  0.0 512.3 jit_solution(13020805028642715624)
XLA Ops:
  8.7 13.2 %all-to-all-start = ((bf16[64,8,1,256]{3,1,2,0:T(8,128)(2,1)}), bf16[64,8,1,256]{3,1,2,0:T(8,128)(2,1)}, u32[]{:S(2)}, u32[]{:S(2)}) async-start(bf16[64,8,1,256]{3,1,2,0:T(8,128)(2,1)} %stack.2), calls=%async_computation | async-start | bytes 524288 | tf_op jit(solution)/shard_map/all_to_all | solution.py:12
  22.0 52.1 %all_gather.18 = bf16[512,640]{1,0:T(8,128)(2,1)S(1)} all-gather(bf16[8,640]{1,0:T(8,128)(2,1)} %param.14), channel_id=1, replica_groups=mesh['req'=64,'tp'=4] {'req'}, dimensions={0}, use_global_device_ids=true | all-gather | bytes 665600 | tf_op jit(solution)/shard_map/all_gather | solution.py:94
  74.0 53.9 %all_gather.19 = bf16[512,640]{1,0:T(8,128)(2,1)} all-gather(bf16[8,640]{1,0:T(8,128)(2,1)} %param.16), channel_id=1, replica_groups=mesh['req'=64,'tp'=4] {'req'}, dimensions={0}, use_global_device_ids=true | all-gather | bytes 665600 | tf_op jit(solution)/shard_map/all_gather | solution.py:96
  128.3 1.7 fusion.69
  131.5 1.6 fusion.33
  134.6 41.7 %all-reduce.2.cloned.1.call-done = f32[8,2560]{1,0:T(8,128)} async-done(((f32[8,2560]{1,0:T(8,128)}), f32[8,2560]{1,0:T(8,128)}) %all-reduce.2.cloned.1.call-update) | async-done | bytes 81936 | tf_op jit(solution)/shard_map/psum | solution.py:112
  178.9 47.8 %all_gather.20 = s32[512,6]{1,0:T(8,128)S(1)} all-gather(s32[8,6]{1,0:T(8,128)S(1)} %copy-done.5), channel_id=1, replica_groups=mesh['req'=64,'tp'=4] {'req'}, dimensions={0}, use_global_device_ids=true | all-gather | bytes 12480 | tf_op jit(solution)/shard_map/all_gather | solution.py:133
  229.9 1.7 fusion.68
  231.8 28.5 %all-gather.3.cloned.1.call-done = bf16[512,2560]{1,0:T(8,128)(2,1)} async-done(((bf16[8,2560]{1,0:T(8,128)(2,1)}), bf16[512,2560]{1,0:T(8,128)(2,1)}) %all-gather.3.cloned.1.call-update) | async-done | bytes 2621456 | tf_op jit(solution)/shard_map/all_gather | solution.py:132
  260.3 3.4 convolution_convert_fusion
  263.7 2.7 reshape.187
  266.4 2.3 fusion.13
  268.7 2.1 fusion.26
  270.8 2.0 convolution_convert_fusion.1
  274.4 6.7 %all-to-all-start.1 = ((bf16[64,2,2560]{2,1,0:T(2,128)(2,1)}), bf16[64,2,2560]{2,1,0:T(2,128)(2,1)}, u32[]{:S(2)}, u32[]{:S(2)}) async-start(bf16[64,2,2560]{2,1,0:T(2,128)(2,1)} %copy.46), calls=%async_computation.1 | async-start | bytes 1310720 | tf_op jit(solution)/shard_map/all_to_all | solution.py:63
  282.1 19.0 %all-to-all-done.1 = bf16[64,2,2560]{2,1,0:T(2,128)(2,1)} async-done(((bf16[64,2,2560]{2,1,0:T(2,128)(2,1)}), bf16[64,2,2560]{2,1,0:T(2,128)(2,1)}, u32[]{:S(2)}, u32[]{:S(2)}) %all-to-all-start.1) | async-done | bytes 655392 | tf_op jit(solution)/shard_map/all_to_all | solution.py:63
  301.2 2.7 reshape.188
  306.5 19.8 %reduce-scatter.4.cloned.1.call-done = bf16[640,8]{1,0:T(8,128)(2,1)} async-done(((bf16[2560,8]{1,0:T(8,128)(2,1)}), bf16[640,8]{1,0:T(8,128)(2,1)}) %reduce-scatter.4.cloned.1.call-update) | async-done | bytes 10256
  328.0 10.3 %all_gather.22 = bf16[8,2560]{1,0:T(8,128)(2,1)} all-gather(bf16[8,640]{1,0:T(8,128)(2,1)S(1)} %add_convert_fusion), channel_id=1, replica_groups=mesh['req'=64,'tp'=4] {'tp'}, dimensions={1}, use_global_device_ids=true | all-gather | bytes 51200 | tf_op jit(solution)/shard_map/all_gather | solution.py:163
  338.4 82.3 %all-gather.5.cloned.1.call-done = bf16[512,2560]{1,0:T(8,128)(2,1)} async-done(((bf16[8,2560]{1,0:T(8,128)(2,1)}), bf16[512,2560]{1,0:T(8,128)(2,1)}) %all-gather.5.cloned.1.call-update) | async-done | bytes 2621456 | tf_op jit(solution)/shard_map/all_gather | solution.py:164
  420.6 2.5 fusion
  423.2 3.0 fusion.20
  426.2 75.4 %pmax.7 = f32[512]{0:T(512)S(1)} all-reduce(f32[512]{0:T(512)S(1)} %fusion.20), channel_id=1, replica_groups=mesh['req'=64,'tp'=4] {'req','tp'}, use_global_device_ids=true, to_apply=%region_15.16 | all-reduce | flops 512 | bytes 4096 | tf_op jit(solution)/shard_map/pmax | solution.py:182
  502.3 2.3 multiply_reduce_fusion
  (77 shorter events, 19.7 us)
Async XLA Ops:
  7.2 125.9 %copy-start = (bf16[640,2560]{1,0:T(8,128)(2,1)S(1)}, bf16[640,2560]{1,0:T(8,128)(2,1)}, u32[]{:S(2)}) copy-start(bf16[640,2560]{1,0:T(8,128)(2,1)} %param.22) | copy-start | bytes 9830404
  7.2 120.8 %copy-start.8 = (s32[512]{0:T(512)S(1)}, s32[512]{0:T(512)}, u32[]{:S(2)}) copy-start(s32[512]{0:T(512)} %param.19) | copy-start | bytes 6148
  7.2 121.0 %copy-start.9 = (s32[8]{0:T(128)S(1)}, s32[8]{0:T(128)}, u32[]{:S(2)}) copy-start(s32[8]{0:T(128)} %param.18) | copy-start | bytes 100
  8.7 121.2 %all-to-all-start = ((bf16[64,8,1,256]{3,1,2,0:T(8,128)(2,1)}), bf16[64,8,1,256]{3,1,2,0:T(8,128)(2,1)}, u32[]{:S(2)}, u32[]{:S(2)}) async-start(bf16[64,8,1,256]{3,1,2,0:T(8,128)(2,1)} %stack.2), calls=%async_computation | async-start | bytes 524288 | tf_op jit(solution)/shard_map/all_to_all | solution.py:12
  21.9 154.3 %all-reduce.2.cloned.1.call-start = ((), (), s32[]{:S(2)}) async-start(), calls=%async_computation.3 | async-start | bytes 163840 | tf_op jit(solution)/shard_map/psum | solution.py:112
  131.5 2.2 copy-start.2
  133.1 44.2 %copy-start.7 = (f32[2560]{0:T(1024)S(1)}, f32[2560]{0:T(1024)}, u32[]{:S(2)}) copy-start(f32[2560]{0:T(1024)} %param.23) | copy-start | bytes 30724
  133.1 45.8 %copy-start.5 = (s32[8,6]{1,0:T(8,128)S(1)}, s32[8,6]{1,0:T(8,128)}, u32[]{:S(2)}) copy-start(s32[8,6]{1,0:T(8,128)} %param.20) | copy-start | bytes 580
  133.9 0.6 copy-start.4
  134.6 125.7 %all-gather.3.cloned.1.call-start = ((), (), s32[]{:S(2)}) async-start(), calls=%async_computation.4 | async-start | bytes 2662400 | tf_op jit(solution)/shard_map/all_gather | solution.py:132
  266.4 2.3 copy-start.3
  270.8 10.9 %copy-start.6 = (f32[8,6]{1,0:T(8,128)S(1)}, f32[8,6]{1,0:T(8,128)}, u32[]{:S(2)}) copy-start(f32[8,6]{1,0:T(8,128)} %param.21) | copy-start | bytes 580
  274.4 26.8 %all-to-all-start.1 = ((bf16[64,2,2560]{2,1,0:T(2,128)(2,1)}), bf16[64,2,2560]{2,1,0:T(2,128)(2,1)}, u32[]{:S(2)}, u32[]{:S(2)}) async-start(bf16[64,2,2560]{2,1,0:T(2,128)(2,1)} %copy.46), calls=%async_computation.1 | async-start | bytes 1310720 | tf_op jit(solution)/shard_map/all_to_all | solution.py:63
  281.1 45.2 %reduce-scatter.4.cloned.1.call-start = ((), (), s32[]{:S(2)}) async-start(), calls=%async_computation.6 | async-start | bytes 819200
  305.3 117.8 %copy-start.10 = (f32[2560]{0:T(1024)S(1)}, f32[2560]{0:T(1024)}, u32[]{:S(2)}) copy-start(f32[2560]{0:T(1024)} %param.26) | copy-start | bytes 30724
  306.5 114.2 %all-gather.5.cloned.1.call-start = ((), (), s32[]{:S(2)}) async-start(), calls=%async_computation.5 | async-start | bytes 2662400 | tf_op jit(solution)/shard_map/all_gather | solution.py:164
  420.6 2.5 copy-start.1
Sparse Core Ops, SparseCore 0:
  134.7 41.5 all-reduce.1
  179.4 80.8 all-gather.2
  306.6 19.6 reduce-scatter.3
  338.4 82.1 all-gather.4
